TPU v7x, 256 devices: a whole 4x4x8 slice. The times are simulated.
256 devices in a mesh: group: 4 (over y), resp: 16 (over z, core), tp: 4 (over x).
Axes of the slice: x: 4, y: 4, z: 8, core: 2. Of those that a mesh axis runs over, the one named last changes fastest.
Arguments:
- query: bfloat16 [16384, 4096], P(('group', 'resp'), 'tp'), parts along dimension 0, may hold values from -150 to 150
- resp_kv: bfloat16 [16384, 2, 1024], P(('group', 'resp'), None, 'tp'), parts along dimension 0, may hold values from -6 to 6
- prefix_kv: bfloat16 [4096, 2, 1024], P(('group', 'resp'), None, 'tp'), parts along dimension 0, may hold values from -6 to 6
- ssm_x: bfloat16 [16384, 8192], P(('group', 'resp'), 'tp'), parts along dimension 0, may hold values from -6 to 6
- bc: bfloat16 [16384, 2, 256], P(('group', 'resp')), parts along dimension 0, may hold values from -1.5 to 1.5
- step_size: float32 [256, 4096], P(('group', 'tp'), 'resp'), parts along dimension 0, may hold values from 0 to 1
- prefix_state: float32 [64, 64, 128, 256], P(('group', 'resp'), 'tp'), parts along dimension 0, may hold values from -1.5 to 1.5
- owner: int32 [256], P(('group', 'tp')), parts along dimension 0, may hold values from 0 to 15
- lengths: int32 [64], P(('group', 'resp')), parts along dimension 0, may hold values from 64 to 256, as said below
- advantage: float32 [64], P(('group', 'resp')), parts along dimension 0, may hold values from -3 to 3
- grad_attn: bfloat16 [16384, 4096], P(('group', 'resp'), 'tp'), parts along dimension 0, may hold values from -6 to 6
- grad_ssm: bfloat16 [16384, 8192], P(('group', 'resp'), 'tp'), parts along dimension 0, may hold values from -6 to 6
Outputs:
- attn_out: bfloat16 [16384, 4096], P(('group', 'resp'), 'tp'), parts along dimension 0
- ssm_out: bfloat16 [16384, 8192], P(('group', 'resp'), 'tp'), parts along dimension 0
- grad_query: bfloat16 [16384, 4096], P(('group', 'resp'), 'tp'), parts along dimension 0
- grad_prefix_kv: bfloat16 [4096, 2, 1024], P(('group', 'resp'), None, 'tp'), parts along dimension 0
- grad_bc: bfloat16 [16384, 2, 256], P(('group', 'resp', 'tp')), parts along dimension 0
- grad_state: float32 [256, 128, 256], P(('group', 'tp')), parts along dimension 0
There are 4 independent parts, one for each index of `group`. A program takes and returns all parts, laid end to end along the dimension named above; each array names one. Nothing has to cross between parts.
Inputs may be any that keep to these rules, and one draw needn't show every extreme that they name: `lengths`: one response of each group has exactly 256 live tokens.
All inputs are finite; a program needn't handle non-finite values.
Results may differ from a plain program's by a relative error of at most 0.025.
Values may be sent and summed in bfloat16 or wider, within the bound.
No kernel may reach another device: no remote copies, remote signals or barrier semaphores. Data moves between devices by JAX's collectives and lax.ppermute only.
A program may use at most 128 MiB of HBM per device.

v0:
```python
import math
import jax
import jax.numpy as jnp
from jax import lax
from jax.sharding import PartitionSpec as P

HEAD_DIM = 128
SSM_DIM = 128
highest = lax.Precision.HIGHEST


def on_device(
    query,
    resp_kv,
    prefix_kv,
    ssm_x,
    bc,
    step_size,
    prefix_state,
    owner,
    lengths,
    advantage,
    grad_attn,
    grad_ssm,
):
    steps_len = query.shape[0]
    kv_local = resp_kv.shape[2] // HEAD_DIM
    group_size = query.shape[1] // resp_kv.shape[2]
    inv_scale = 1.0 / math.sqrt(HEAD_DIM)
    positions = jnp.arange(steps_len)
    causal = positions[None, :] <= positions[:, None]
    factor = advantage[0] * steps_len / lengths[0].astype(jnp.float32)
    alive_rows = (positions < lengths[0]).astype(jnp.float32) * factor
    grad_out = (alive_rows[:, None] * grad_attn.astype(jnp.float32)).astype(jnp.bfloat16)
    grad_y = (alive_rows[:, None] * grad_ssm.astype(jnp.float32)).astype(jnp.bfloat16)
    cache = lax.all_gather(prefix_kv, "resp", axis=0, tiled=True)
    prefix_count = cache.shape[0]
    query_heads = query.reshape(steps_len, kv_local, group_size, HEAD_DIM)
    grad_heads = grad_out.reshape(steps_len, kv_local, group_size, HEAD_DIM)
    prefix_keys = cache[:, 0].reshape(prefix_count, kv_local, HEAD_DIM)
    prefix_values = cache[:, 1].reshape(prefix_count, kv_local, HEAD_DIM)
    own_keys = resp_kv[:, 0].reshape(steps_len, kv_local, HEAD_DIM)
    own_values = resp_kv[:, 1].reshape(steps_len, kv_local, HEAD_DIM)
    prefix_scores = (
        jnp.einsum("tgid,kgd->gitk", query_heads, prefix_keys, preferred_element_type=jnp.float32)
        * inv_scale
    )
    own_scores = jnp.where(
        causal,
        jnp.einsum("tgid,kgd->gitk", query_heads, own_keys, preferred_element_type=jnp.float32)
        * inv_scale,
        -jnp.inf,
    )
    row_top = jnp.maximum(jnp.max(prefix_scores, -1), jnp.max(own_scores, -1))
    row_total = jnp.sum(jnp.exp(prefix_scores - row_top[..., None]), -1) + jnp.sum(
        jnp.exp(own_scores - row_top[..., None]), -1
    )
    log_total = row_top + jnp.log(row_total)
    prefix_weights = jnp.exp(prefix_scores - log_total[..., None]).astype(jnp.bfloat16)
    own_weights = jnp.exp(own_scores - log_total[..., None]).astype(jnp.bfloat16)
    attended = jnp.einsum(
        "gitk,kgd->tgid", prefix_weights, prefix_values, preferred_element_type=jnp.float32
    ) + jnp.einsum("gitk,kgd->tgid", own_weights, own_values, preferred_element_type=jnp.float32)
    attn_out = attended.reshape(steps_len, -1).astype(jnp.bfloat16)
    row_delta = jnp.transpose(jnp.sum(grad_heads.astype(jnp.float32) * attended, -1), (1, 2, 0))
    prefix_slope = jnp.einsum(
        "tgid,kgd->gitk", grad_heads, prefix_values, preferred_element_type=jnp.float32
    )
    own_slope = jnp.einsum(
        "tgid,kgd->gitk", grad_heads, own_values, preferred_element_type=jnp.float32
    )
    prefix_score_grad = (
        prefix_weights.astype(jnp.float32) * (prefix_slope - row_delta[..., None]) * inv_scale
    ).astype(jnp.bfloat16)
    own_score_grad = (
        own_weights.astype(jnp.float32) * (own_slope - row_delta[..., None]) * inv_scale
    ).astype(jnp.bfloat16)
    grad_query = (
        (
            jnp.einsum(
                "gitk,kgd->tgid", prefix_score_grad, prefix_keys, preferred_element_type=jnp.float32
            )
            + jnp.einsum(
                "gitk,kgd->tgid", own_score_grad, own_keys, preferred_element_type=jnp.float32
            )
        )
        .reshape(steps_len, -1)
        .astype(jnp.bfloat16)
    )
    block_rows = prefix_kv.shape[0]
    grad_keys = jnp.einsum(
        "gitk,tgid->kgd", prefix_score_grad, query_heads, preferred_element_type=jnp.float32
    )
    grad_values = jnp.einsum(
        "gitk,tgid->kgd", prefix_weights, grad_heads, preferred_element_type=jnp.float32
    )
    grad_prefix_kv = lax.psum_scatter(
        jnp.stack(
            [
                grad_keys.reshape(lax.axis_size("resp") * block_rows, -1),
                grad_values.reshape(lax.axis_size("resp") * block_rows, -1),
            ],
            axis=1,
        ).astype(jnp.bfloat16),
        "resp",
        scatter_dimension=0,
        tiled=True,
    )
    heads_local = step_size.shape[0]
    head_inputs = ssm_x.reshape(steps_len, heads_local, SSM_DIM)
    input_maps = bc[:, 0]
    read_maps = bc[:, 1]
    read_wide = read_maps.astype(jnp.float32)
    cumulative = jnp.cumsum(step_size, axis=1)
    segment = jnp.exp(
        jnp.where(causal[None], cumulative[:, None, :] - cumulative[:, :, None], -jnp.inf)
    )
    pair_inner = jnp.dot(read_maps, input_maps.T, preferred_element_type=jnp.float32)
    mixing = (segment * step_size[:, None, :] * pair_inner[None]).astype(jnp.bfloat16)
    from_inputs = jnp.einsum(
        "hts,shp->thp", mixing, head_inputs, preferred_element_type=jnp.float32
    )
    held_here = (owner == lax.axis_index("resp"))[:, None, None]
    own_slot = jnp.where(held_here, prefix_state[0], jnp.zeros_like(prefix_state[0]))
    start_state = lax.psum(own_slot.astype(jnp.bfloat16), "resp").astype(jnp.float32)
    carried = jnp.exp(-cumulative)
    from_state = (
        jnp.einsum("tn,hpn->thp", read_wide, start_state, precision=highest) * carried.T[:, :, None]
    )
    ssm_out = (from_inputs + from_state).reshape(steps_len, -1).astype(jnp.bfloat16)
    grad_heads_y = grad_y.reshape(steps_len, heads_local, SSM_DIM)
    inner_grad = jnp.einsum(
        "thp,shp->hts", grad_heads_y, head_inputs, preferred_element_type=jnp.float32
    )
    grad_mix = (segment * step_size[:, None, :] * inner_grad).astype(jnp.bfloat16)
    weighted = grad_heads_y.astype(jnp.float32) * carried.T[:, :, None]
    grad_read = jnp.einsum(
        "hts,sn->tn", grad_mix, input_maps, preferred_element_type=jnp.float32
    ) + jnp.einsum("thp,hpn->tn", weighted, start_state, precision=highest)
    grad_input = jnp.einsum("hts,tn->sn", grad_mix, read_maps, preferred_element_type=jnp.float32)
    state_term = jnp.einsum("thp,tn->hpn", weighted, read_wide, precision=highest)
    grad_state = lax.psum(state_term.astype(jnp.bfloat16), "resp").astype(jnp.float32)
    map_terms = jnp.stack([grad_input, grad_read], axis=1)
    whole_sum = lax.psum(map_terms.astype(jnp.bfloat16), "tp").astype(jnp.float32)
    share_rows = steps_len // lax.axis_size("tp")
    grad_bc = lax.dynamic_slice_in_dim(
        whole_sum, lax.axis_index("tp") * share_rows, share_rows, 0
    ).astype(jnp.bfloat16)
    return (attn_out, ssm_out, grad_query, grad_prefix_kv, grad_bc, grad_state)


def solution(mesh):
    return jax.shard_map(
        on_device,
        mesh=mesh,
        in_specs=(
            P(("group", "resp"), "tp"),
            P(("group", "resp"), None, "tp"),
            P(("group", "resp"), None, "tp"),
            P(("group", "resp"), "tp"),
            P(("group", "resp"), None, None),
            P(("group", "tp"), "resp"),
            P(("group", "resp"), "tp", None, None),
            P(("group", "tp")),
            P(("group", "resp")),
            P(("group", "resp")),
            P(("group", "resp"), "tp"),
            P(("group", "resp"), "tp"),
        ),
        out_specs=(
            P(("group", "resp"), "tp"),
            P(("group", "resp"), "tp"),
            P(("group", "resp"), "tp"),
            P(("group", "resp"), None, "tp"),
            P(("group", "resp", "tp"), None, None),
            P(("group", "tp"), None, None),
        ),
        check_vma=False,
    )
```

profile of v0, /device:TPU:8, one launch (start us, length us, event | category | flops | bytes accessed | tf_op | source)
XLA Modules:
  0.0 269.7 jit_solution(11355581099030665395)
XLA Ops:
  7.2 0.0 all-gather.2.cloned.1.call-start
  7.2 0.7 all-gather.2.cloned.1.call-update
  7.9 0.0 all-reduce.7.cloned.1.call-start
  9.3 0.7 copy_bitcast_fusion.4
  10.0 0.6 reduce-window.6
  10.5 0.2 slice_reduce_fusion
  10.8 0.1 exponential_bitcast_fusion
  10.8 0.2 mul.110
  11.0 1.8 copy.121
  12.9 3.2 %convert_multiply_fusion = (f32[256,2048]{1,0:T(8,128)S(1)}, bf16[256,2048]{1,0:T(8,128)(2,1)}) fusion(f32[256,2048]{1,0:T(8,128)} %copy.121, bf16[256,2048]{1,0:T(8,128)(2,1)} %param.23, f32[256]{0:T(256)S(1)} %compare_select_fusion), kind=kLoop, calls=%fused_computation.26 | loop fusion | flops 2621440 | bytes 6292480 | tf_op jit(solution)/shard_map/mul | solution.py:136
  16.1 1.2 fusion.53
  17.2 1.1 copy.159
  18.3 2.0 copy.162
  20.3 2.0 multiply_convert_fusion.4
  22.3 2.0 copy.103
  24.4 1.1 copy.95
  25.4 1.8 copy.157
  27.3 2.3 fusion.52
  29.6 1.3 copy.117
  30.9 0.8 copy.97
  31.7 0.7 copy_bitcast_fusion.3
  32.4 1.5 fusion.54
  34.0 1.3 fusion.13
  35.3 0.7 copy-done.5
  35.9 2.1 convolution_convert_fusion
  38.0 13.4 %all-gather.2.cloned.1.call-done = bf16[1024,2,256]{2,1,0:T(2,128)(2,1)} async-done(((bf16[64,2,256]{2,1,0:T(2,128)(2,1)}), bf16[1024,2,256]{2,1,0:T(2,128)(2,1)}) %all-gather.2.cloned.1.call-update) | async-done | bytes 1048592 | tf_op jit(solution)/shard_map/all_gather | solution.py:36
  51.4 4.3 %fusion.51 = (bf16[1024,1,256]{2,1,0:T(2,128)(2,1)}, bf16[1024,1,256]{2,1,0:T(2,128)(2,1)}) fusion(bf16[1024,2,256]{2,1,0:T(2,128)(2,1)} %all-gather.2.cloned.1.call-done), kind=kLoop, calls=%fused_computation.85 | loop fusion | bytes 2097152 | tf_op jit(solution)/shard_map/slice | solution.py:40
  55.7 3.5 %copy.158 = bf16[1024,1,256]{0,2,1:T(8,128)(2,1)} copy(bf16[1024,1,256]{2,1,0:T(2,128)(2,1)} %get-tuple-element.31) | data formatting | bytes 1048576
  59.2 2.5 bitcast_reduce_fusion
  61.8 0.3 exponential_reduce_fusion
  62.1 1.4 fusion.4
  63.5 3.4 %fusion.6 = bf16[2,4,256,1024]{2,3,1,0:T(8,128)(2,1)} fusion(f32[2,1024,256,4]{2,1,3,0:T(8,128)S(1)} %get-tuple-element.38, f32[2,4,256]{2,1,0:T(4,128)S(1)} %bitcast.215), kind=kLoop, calls=%fused_computation.10 | loop fusion | flops 6291456 | bytes 12591104 | tf_op jit(solution)/shard_map/convert_element_type | solution.py:59
  66.8 3.5 %copy.93 = bf16[1024,1,256]{0,2,1:T(8,128)(2,1)} copy(bf16[1024,1,256]{2,1,0:T(2,128)(2,1)} %get-tuple-element.32) | data formatting | bytes 1048576 | tf_op jit(solution)/shard_map/slice | solution.py:41
  70.3 3.2 %fusion.55 = f32[2,4,256,128]{2,3,1,0:T(8,128)S(1)} fusion(bf16[1024,2,128,1]{0,2,3,1:T(8,128)(2,1)} %bitcast.202, bf16[2,4,256,1024]{2,3,1,0:T(8,128)(2,1)} %fusion.6), kind=kOutput, calls=%fused_computation.89 | convolution fusion | flops 536870912 | bytes 5767168 | tf_op jit(solution)/shard_map/gitk,kgd->tgid/dot_general | solution.py:61
  73.5 0.4 copy-done.1
  73.9 0.1 copy-done.4
  74.0 2.3 fusion.28
  76.4 1.3 multiply_reduce_fusion
  77.7 1.8 fusion.2
  79.5 2.3 fusion.27
  81.8 3.6 %copy.115 = bf16[1024,1,256]{2,1,0:T(2,128)(2,1)} copy(bf16[1024,1,256]{0,2,1:T(8,128)(2,1)} %bitcast.206) | data formatting | bytes 1048576 | tf_op jit(solution)/shard_map/stack;reshape | solution.py:98
  85.3 3.6 %copy.116 = bf16[1024,1,256]{2,1,0:T(2,128)(2,1)} copy(bf16[1024,1,256]{0,2,1:T(8,128)(2,1)} %bitcast.205) | data formatting | bytes 1048576 | tf_op jit(solution)/shard_map/stack;reshape | solution.py:98
  88.9 4.2 %pad_maximum_fusion = bf16[1024,2,256]{2,1,0:T(2,128)(2,1)} fusion(bf16[1024,1,256]{2,1,0:T(2,128)(2,1)} %copy.116, bf16[1024,1,256]{2,1,0:T(2,128)(2,1)} %copy.115), kind=kLoop, calls=%fused_computation.57 | loop fusion | flops 2097152 | bytes 2097152 | tf_op jit(solution)/shard_map/stack | solution.py:98
  93.1 0.0 all-reduce.5.cloned.1.call-start
  93.2 3.4 %convert_reduce_fusion = bf16[256,256]{1,0:T(8,128)(2,1)} fusion(bf16[256,16,128]{0,2,1:T(8,128)(2,1)} %bitcast.213, f32[16,256]{1,0:T(8,128)} %param.17, f32[16,256]{1,0:T(8,128)} %copy_bitcast_fusion.3, pred[256,256]{1,0:T(8,128)(4,1)} %copy.97, bf16[256,2048]{1,0:T(8,128)(2,1)S(1)} %copy-done), kind=kOutput, calls=%fused_computation.11 | convolution fusion | flops 275709952 | bytes 2326528 | tf_op jit(solution)/shard_map/thp,shp->hts/dot_general | solution.py:132
  96.6 1.3 dynamic-slice
  98.5 1.8 fusion.33
  100.3 1.2 fusion.47
  101.5 4.1 %fusion.7 = f32[16,256,128]{1,2,0:T(8,128)} fusion(f32[256,256]{1,0:T(8,128)S(1)} %fusion.47, f32[16,256]{1,0:T(8,128)} %param.17, f32[16,256]{1,0:T(8,128)} %copy_bitcast_fusion.3, pred[256,256]{1,0:T(8,128)(4,1)} %copy.97, bf16[256,2048]{1,0:T(8,128)(2,1)S(1)} %copy-done), kind=kOutput, calls=%fused_computation.15 | convolution fusion | flops 273678336 | bytes 3506176 | tf_op jit(solution)/shard_map/hts,shp->thp/dot_general | solution.py:120
  105.6 1.7 fusion.56
  107.3 3.1 %fusion.26 = bf16[2,4,256,128]{2,3,1,0:T(8,128)(2,1)} fusion(f32[2,4,256,128]{2,3,1,0:T(8,128)} %fusion.56, bf16[256,2,128,1]{0,2,3,1:T(8,128)(2,1)S(1)} %bitcast.210, bf16[256,2,4,128]{0,3,2,1:T(8,128)(2,1)} %bitcast.192, bf16[256,2,128,1]{0,2,3,1:T(8,128)(2,1)S(1)} %bitcast.212, f32[2,4,256]{2,1,0:T(4,128)S(1)} %bitcast.220, ...), kind=kOutput, calls=%fused_computation.46 | convolution fusion | flops 272629760 | bytes 4472832 | tf_op jit(solution)/shard_map/gitk,kgd->tgid/dot_general | solution.py:83
  110.4 2.2 copy.125
  112.5 2.1 copy.123
  114.6 96.1 %all-reduce.7.cloned.1.call-done = (bf16[16,128,256]{2,1,0:T(8,128)(2,1)}, bf16[1024,2,256]{2,1,0:T(2,128)(2,1)}, bf16[16,128,256]{2,1,0:T(8,128)(2,1)}) async-done(((bf16[16,128,256]{2,1,0:T(8,128)(2,1)}, bf16[1024,2,256]{2,1,0:T(2,128)(2,1)}, bf16[16,128,256]{2,1,0:T(8,128)(2,1)}), (bf16[16,128,256]{2,1,0:T(8,128)(2,1)}, bf16[1024,2,256]{2,1,0:T(2,128)(2,1)}, ...) | async-done | bytes 3145744 | tf_op jit(solution)/shard_map/psum | solution.py:125
  210.7 3.0 %fusion.29 = f32[256,256]{1,0:T(8,128)S(1)} fusion(bf16[16,128,256]{2,1,0:T(8,128)(2,1)} %get-tuple-element.24, bf16[256,16,128]{0,2,1:T(8,128)(2,1)S(1)} %bitcast.214, f32[256,16]{0,1:T(8,128)S(1)} %copy-done.19), kind=kOutput, calls=%fused_computation.50 | convolution fusion | flops 1611661312 | bytes 2375680 | tf_op jit(solution)/shard_map/thp,hpn->tn/dot_general | solution.py:139
  213.8 0.2 fusion.34
  214.0 0.7 pad_maximum_fusion.1
  214.8 2.5 fusion.12
  217.2 1.5 convert_element_type.121
  218.8 1.4 copy.124
  220.2 1.5 constant_dynamic-slice_fusion
  221.7 39.9 %all-reduce.5.cloned.1.call-done = bf16[256,2,256]{2,0,1:T(8,128)(2,1)} async-done(((bf16[256,2,256]{2,0,1:T(8,128)(2,1)}), bf16[256,2,256]{2,0,1:T(8,128)(2,1)}) %all-reduce.5.cloned.1.call-update) | async-done | bytes 262160 | tf_op jit(solution)/shard_map/psum | solution.py:144
  261.6 0.8 convert_convert_fusion
  262.4 0.7 copy.126
  (53 shorter events, 0.2 us)
Async XLA Ops:
  7.2 86.0 %copy-start = (bf16[256,2048]{1,0:T(8,128)(2,1)S(1)}, bf16[256,2048]{1,0:T(8,128)(2,1)}, u32[]{:S(2)}) copy-start(bf16[256,2048]{1,0:T(8,128)(2,1)} %param.15) | copy-start | bytes 3145732
  7.2 44.2 %all-gather.2.cloned.1.call-start = ((), (), s32[]{:S(2)}) async-start(), calls=%async_computation | async-start | bytes 1114112 | tf_op jit(solution)/shard_map/all_gather | solution.py:36
  7.9 202.8 %all-reduce.7.cloned.1.call-start = ((), (), s32[]{:S(2)}) async-start(), calls=%async_computation.2 | async-start | bytes 6291456 | tf_op jit(solution)/shard_map/psum | solution.py:125
  10.7 2.1 copy-start.20
  10.8 2.0 copy-start.18
  12.9 3.2 %copy-start.13 = (bf16[256,2,256]{2,1,0:T(2,128)(2,1)S(1)}, bf16[256,2,256]{2,1,0:T(2,128)(2,1)}, u32[]{:S(2)}) copy-start(bf16[256,2,256]{2,1,0:T(2,128)(2,1)} %param.13) | copy-start | bytes 786436
  27.3 2.3 copy-start.9
  27.3 4.5 %copy-start.22 = (s32[16]{0:T(128)S(1)}, s32[16]{0:T(128)}, u32[]{:S(2)}) copy-start(s32[16]{0:T(128)} %param.19) | copy-start | bytes 196
  27.3 4.5 %copy-start.21 = (f32[16,2]{0,1:T(2,128)S(1)}, f32[16,2]{0,1:T(2,128)}, u32[]{:S(2)}) copy-start(f32[16,2]{0,1:T(2,128)} %copy-done.20) | copy-start | bytes 388
  30.9 1.5 copy-start.15
  31.7 2.3 copy-start.10
  34.0 2.0 copy-start.5
  70.3 3.6 %copy-start.1 = (bf16[2,4,256,1024]{2,3,1,0:T(8,128)(2,1)S(1)}, bf16[2,4,256,1024]{2,3,1,0:T(8,128)(2,1)}, u32[]{:S(2)}) copy-start(bf16[2,4,256,1024]{2,3,1,0:T(8,128)(2,1)} %fusion.6) | copy-start | bytes 12582916
  70.3 3.7 %copy-start.4 = (bf16[256,1024]{0,1:T(8,128)(2,1)S(1)}, bf16[256,1024]{0,1:T(8,128)(2,1)}, u32[]{:S(2)}) copy-start(bf16[256,1024]{0,1:T(8,128)(2,1)} %copy.103) | copy-start | bytes 1572868
  76.4 1.3 copy-start.8
  77.7 1.8 copy-start.6
  79.5 2.3 copy-start.2
  93.1 168.5 %all-reduce.5.cloned.1.call-start = ((), (), s32[]{:S(2)}) async-start(), calls=%async_computation.1 | async-start | bytes 524288 | tf_op jit(solution)/shard_map/psum | solution.py:144
  101.5 4.1 %copy-start.3 = (bf16[2,4,256,1024]{2,3,1,0:T(8,128)(2,1)S(1)}, bf16[2,4,256,1024]{2,3,1,0:T(8,128)(2,1)}, u32[]{:S(2)}) copy-start(bf16[2,4,256,1024]{2,3,1,0:T(8,128)(2,1)} %copy-done.2) | copy-start | bytes 12582916
  101.5 4.1 %copy-start.7 = (bf16[1024,1,256]{0,2,1:T(8,128)(2,1)S(1)}, bf16[1024,1,256]{0,2,1:T(8,128)(2,1)}, u32[]{:S(2)}) copy-start(bf16[1024,1,256]{0,2,1:T(8,128)(2,1)} %copy.158) | copy-start | bytes 1572868
  110.4 100.3 %copy-start.12 = (bf16[256,2048]{0,1:T(8,128)(2,1)S(1)}, bf16[256,2048]{0,1:T(8,128)(2,1)}, u32[]{:S(2)}) copy-start(bf16[256,2048]{0,1:T(8,128)(2,1)} %copy.117) | copy-start | bytes 3145732
  110.4 100.3 %copy-start.19 = (f32[256,16]{0,1:T(8,128)S(1)}, f32[256,16]{0,1:T(8,128)}, u32[]{:S(2)}) copy-start(f32[256,16]{0,1:T(8,128)} %copy-done.18) | copy-start | bytes 49156
  110.4 103.4 %copy-start.14 = (bf16[256,1,256]{2,1,0:T(2,128)(2,1)S(1)}, bf16[256,1,256]{2,1,0:T(2,128)(2,1)}, u32[]{:S(2)}) copy-start(bf16[256,1,256]{2,1,0:T(2,128)(2,1)} %get-tuple-element.33) | copy-start | bytes 393220
  110.4 103.4 %copy-start.16 = (bf16[256,256]{1,0:T(8,128)(2,1)S(1)}, bf16[256,256]{1,0:T(8,128)(2,1)}, u32[]{:S(2)}) copy-start(bf16[256,256]{1,0:T(8,128)(2,1)} %convert_reduce_fusion) | copy-start | bytes 393220
  112.5 101.4 %copy-start.17 = (bf16[256,1,256]{2,0,1:T(8,128)(2,1)S(1)}, bf16[256,1,256]{2,0,1:T(8,128)(2,1)}, u32[]{:S(2)}) copy-start(bf16[256,1,256]{2,0,1:T(8,128)(2,1)} %fusion.33) | copy-start | bytes 393220
  214.7 2.5 copy-start.11
Sparse Core Ops, SparseCore 0:
  9.8 41.4 all-gather.1
  93.2 117.4 all-reduce.6
  214.9 46.6 all-reduce.4
where the time goes:
time: 271 us; the launch traced here: 270 us
  waiting for transfers between devices  150 us (55%)
  local copies, waits for them, and re-layouts  45.2 us (17%)
  matrix products  38 us (14%)
  other arithmetic  20.2 us (7%)
  between operations  16 us (6%)
    psum x1, waiting for transfers between devices, on_device(): lax.psum(own_slot.astype(jnp.bfloat16), 'resp').astype(jnp.float32)  96.1 us
    psum x1, waiting for transfers between devices, on_device(): lax.psum(map_terms.astype(jnp.bfloat16), 'tp').astype(jnp.float32)  39.9 us
    unnamed x55, local copies, waits for them, and re-layouts  15 us
    all_gather x1, waiting for transfers between devices, on_device(): cache = lax.all_gather(prefix_kv, 'resp', axis=0, tiled=True)  13.4 us
    another operation x2, local copies, waits for them, and re-layouts, on_device(): jnp.stack([grad_keys.reshape(lax.axis_size('resp') * block_rows, -1), gra...  7.11 us
  transfers between devices with their start and end apart: 3, of which 3 were waited for; matrix products, arithmetic and copies ran while one was open for 21% of the time, Pallas kernels for 0%

commit v1 on v0

--- a/solution.py
+++ b/solution.py
@@ -23,6 +23,11 @@
     grad_attn,
     grad_ssm,
 ):
+
+    def _resolve_edge(array_in):
+        b_now = jnp.sum(lax.all_gather(array_in, axis_name="resp"), axis=0)
+        return b_now
+
     steps_len = query.shape[0]
     kv_local = resp_kv.shape[2] // HEAD_DIM
     group_size = query.shape[1] // resp_kv.shape[2]
@@ -122,7 +127,7 @@
     )
     held_here = (owner == lax.axis_index("resp"))[:, None, None]
     own_slot = jnp.where(held_here, prefix_state[0], jnp.zeros_like(prefix_state[0]))
-    start_state = lax.psum(own_slot.astype(jnp.bfloat16), "resp").astype(jnp.float32)
+    start_state = _resolve_edge(own_slot.astype(jnp.bfloat16)).astype(jnp.float32)
     carried = jnp.exp(-cumulative)
     from_state = (
         jnp.einsum("tn,hpn->thp", read_wide, start_state, precision=highest) * carried.T[:, :, None]

time: 271 us -> 375 us (1.38)
  waiting for transfers between devices: 150 us -> 244 us
  other arithmetic: 20.2 us -> 30.8 us
  matrix products: 38 us -> 34.1 us
  local copies, waits for them, and re-layouts: 45.2 us -> 49.1 us
    psum x1 -> x0, waiting for transfers between devices: 96.1 us -> none  [on_device(): lax.psum(own_slot.astype(jnp.bfloat16), 'resp').astype(jnp.float32)]
    all_gather x0 -> x1, waiting for transfers between devices: none -> 93.6 us  [_resolve_edge(): b_now = jnp.sum(lax.all_gather(array_in, axis_name='resp'), axis=0)]
    unnamed x3 -> x5, waiting for transfers between devices: 0.71 us -> 89.2 us
    reduce_sum x0 -> x1, other arithmetic: none -> 8.93 us  [_resolve_edge(): b_now = jnp.sum(lax.all_gather(array_in, axis_name='resp'), axis=0)]
    all_gather x1, waiting for transfers between devices: 13.4 us -> 18.8 us  [on_device(): cache = lax.all_gather(prefix_kv, 'resp', axis=0, tiled=True)]
    unnamed x55 -> x67, local copies, waits for them, and re-layouts: 15 us -> 17.3 us
  transfers between devices with their start and end apart: 3 -> 4, of which waited for: 3 -> 4; matrix products, arithmetic and copies ran while one was open for 21% -> 15% of each run, Pallas kernels for 0% -> 0%
where the time goes in v1:
time: 375 us; the launch traced here: 374 us
  waiting for transfers between devices  244 us (65%)
  local copies, waits for them, and re-layouts  49.1 us (13%)
  matrix products  34.1 us (9%)
  other arithmetic  30.8 us (8%)
  between operations  16.2 us (4%)
    all_gather x1, waiting for transfers between devices, _resolve_edge(): b_now = jnp.sum(lax.all_gather(array_in, axis_name='resp'), axis=0)  93.6 us
    unnamed x5, waiting for transfers between devices  89.2 us
    psum x1, waiting for transfers between devices, on_device(): lax.psum(map_terms.astype(jnp.bfloat16), 'tp').astype(jnp.float32)  42 us
    all_gather x1, waiting for transfers between devices, on_device(): cache = lax.all_gather(prefix_kv, 'resp', axis=0, tiled=True)  18.8 us
    unnamed x67, local copies, waits for them, and re-layouts  17.3 us
    reduce_sum x1, other arithmetic, _resolve_edge(): b_now = jnp.sum(lax.all_gather(array_in, axis_name='resp'), axis=0)  8.93 us
  transfers between devices with their start and end apart: 4, of which 4 were waited for; matrix products, arithmetic and copies ran while one was open for 15% of the time, Pallas kernels for 0%

profile of v1, /device:TPU:8, one launch (start us, length us, event | category | flops | bytes accessed | tf_op | source)
XLA Modules:
  0.0 373.8 jit_solution(206731154105567308)
XLA Ops:
  7.2 0.7 all-gather.3.cloned.1.call-update
  9.3 0.7 copy_bitcast_fusion.4
  10.0 0.6 reduce-window.6
  10.6 0.2 slice_reduce_fusion
  10.8 2.0 copy.162
  12.9 1.2 multiply_convert_fusion.4
  14.1 1.0 copy.103
  15.1 1.5 fusion.52
  16.6 0.1 copy.95
  16.8 0.1 copy.159
  16.9 1.1 fusion.51
  18.0 0.1 exponential_bitcast_fusion
  18.1 1.5 mul.110
  19.6 1.9 copy.121
  21.5 3.2 convert_multiply_fusion
  24.7 2.9 copy.157
  27.7 0.6 copy-done.15
  28.3 2.1 fusion.53
  30.5 2.1 convolution_convert_fusion
  32.6 18.8 %all-gather.3.cloned.1.call-done = bf16[1024,2,256]{2,1,0:T(2,128)(2,1)} async-done(((bf16[64,2,256]{2,1,0:T(2,128)(2,1)}), bf16[1024,2,256]{2,1,0:T(2,128)(2,1)}) %all-gather.3.cloned.1.call-update) | async-done | bytes 1048592 | tf_op jit(solution)/shard_map/all_gather | solution.py:41
  51.4 4.3 %fusion.50 = (bf16[1024,1,256]{2,1,0:T(2,128)(2,1)}, bf16[1024,1,256]{2,1,0:T(2,128)(2,1)}) fusion(bf16[1024,2,256]{2,1,0:T(2,128)(2,1)} %all-gather.3.cloned.1.call-done), kind=kLoop, calls=%fused_computation.84 | loop fusion | bytes 2097152 | tf_op jit(solution)/shard_map/slice | solution.py:45
  55.7 3.5 copy.158
  59.2 3.5 copy.93
  62.7 2.5 bitcast_reduce_fusion
  65.3 0.3 exponential_reduce_fusion
  65.6 1.4 fusion.4
  67.0 1.5 fusion.6
  68.5 1.9 copy-done.1
  70.4 2.3 fusion.27
  72.7 3.6 copy.116
  76.2 3.2 fusion.54
  79.5 1.3 multiply_reduce_fusion
  80.8 1.8 fusion.2
  82.6 1.9 copy-done.3
  84.6 2.3 fusion.26
  86.9 3.6 copy.115
  90.4 4.2 %pad_maximum_fusion = bf16[1024,2,256]{2,1,0:T(2,128)(2,1)} fusion(bf16[1024,1,256]{2,1,0:T(2,128)(2,1)} %copy.116, bf16[1024,1,256]{2,1,0:T(2,128)(2,1)} %copy.115), kind=kLoop, calls=%fused_computation.56 | loop fusion | flops 2097152 | bytes 2097152 | tf_op jit(solution)/shard_map/stack | solution.py:103
  94.7 0.7 broadcast_compare_fusion
  95.3 2.8 select_convert_fusion
  98.3 1.6 copy.97
  99.9 2.3 copy.117
  102.1 1.3 dynamic-slice
  104.0 0.7 copy_bitcast_fusion.3
  104.8 2.8 convert_reduce_fusion
  107.6 0.9 fusion.32
  108.5 0.2 fusion.46
  108.7 2.8 fusion.7
  111.6 1.7 fusion.55
  113.3 3.1 fusion.25
  116.3 2.0 copy.125
  118.4 2.0 copy.123
  120.4 88.4 %all-reduce.7.cloned.1.call-done = (bf16[1024,2,256]{2,1,0:T(2,128)(2,1)}, bf16[16,128,256]{2,1,0:T(8,128)(2,1)}) async-done(((bf16[1024,2,256]{2,1,0:T(2,128)(2,1)}, bf16[16,128,256]{2,1,0:T(8,128)(2,1)}), (bf16[1024,2,256]{2,1,0:T(2,128)(2,1)}, bf16[16,128,256]{2,1,0:T(8,128)(2,1)})) %all-reduce.7.cloned.1.call-update) | async-done | bytes 2097168
  208.9 2.8 convert_element_type.124
  211.6 1.5 constant_dynamic-slice_fusion
  213.2 93.6 %all-gather.5.cloned.1.call-done = bf16[16,16,128,256]{3,2,1,0:T(8,128)(2,1)} async-done(((bf16[1,16,128,256]{3,2,1,0:T(8,128)(2,1)}), bf16[16,16,128,256]{3,2,1,0:T(8,128)(2,1)}) %all-gather.5.cloned.1.call-update) | async-done | bytes 16777232 | tf_op jit(solution)/shard_map/all_gather | solution.py:28
  306.8 8.9 %reduce_sum.54 = bf16[16,128,256]{2,1,0:T(8,128)(2,1)S(1)} reduce(bf16[16,16,128,256]{3,2,1,0:T(8,128)(2,1)} %all-gather.5.cloned.1.call-done, bf16[]{:T(256)} %constant.26.clone.1), dimensions={0}, to_apply=%region_6.7 | reduce | flops 7864320 | bytes 17825794 | tf_op jit(solution)/shard_map/reduce_sum | solution.py:28
  315.7 1.8 fusion.28
  317.6 1.1 fusion.33
  318.7 1.6 pad_maximum_fusion.1
  320.3 2.1 fusion.12
  322.4 1.4 copy.124
  323.8 42.0 %all-reduce.5.cloned.1.call-done = bf16[256,2,256]{2,0,1:T(8,128)(2,1)} async-done(((bf16[256,2,256]{2,0,1:T(8,128)(2,1)}), bf16[256,2,256]{2,0,1:T(8,128)(2,1)}) %all-reduce.5.cloned.1.call-update) | async-done | bytes 262160 | tf_op jit(solution)/shard_map/psum | solution.py:149
  365.8 0.8 convert_convert_fusion
  366.6 0.7 copy.126
  (69 shorter events, 0.4 us)
Async XLA Ops:
  7.2 97.6 %copy-start = (bf16[256,2048]{1,0:T(8,128)(2,1)S(1)}, bf16[256,2048]{1,0:T(8,128)(2,1)}, u32[]{:S(2)}) copy-start(bf16[256,2048]{1,0:T(8,128)(2,1)} %param.15) | copy-start | bytes 3145732
  7.2 9.8 %copy-start.12 = (bf16[256,2,256]{2,1,0:T(2,128)(2,1)S(1)}, bf16[256,2,256]{2,1,0:T(2,128)(2,1)}, u32[]{:S(2)}) copy-start(bf16[256,2,256]{2,1,0:T(2,128)(2,1)} %param.16) | copy-start | bytes 786436
  7.2 44.2 %all-gather.3.cloned.1.call-start = ((), (), s32[]{:S(2)}) async-start(), calls=%async_computation | async-start | bytes 1114112 | tf_op jit(solution)/shard_map/all_gather | solution.py:41
  7.9 200.9 %all-reduce.7.cloned.1.call-start = ((), (), s32[]{:S(2)}) async-start(), calls=%async_computation.3 | async-start | bytes 4194304
  10.8 8.8 %copy-start.27 = (f32[16,2]{0,1:T(2,128)}, f32[16,2]{0,1:T(2,128)S(1)}, u32[]{:S(2)}) copy-start(f32[16,2]{0,1:T(2,128)S(1)} %slice.29) | copy-start | bytes 388
  12.9 3.9 %copy-start.28 = (f32[256]{0:T(256)}, f32[256]{0:T(256)S(1)}, u32[]{:S(2)}) copy-start(f32[256]{0:T(256)S(1)} %compare_select_fusion) | copy-start | bytes 3076
  18.1 1.5 copy-start.17
  27.6 2.8 copy-start.7
  27.7 0.6 copy-start.15
  62.7 2.5 copy-start.25
  67.0 1.5 copy-start.19
  67.0 3.4 copy-start.5
  68.4 1.9 copy-start.1
  76.2 3.2 copy-start.6
  76.2 3.2 copy-start.20
  76.2 4.6 %copy-start.2 = (bf16[2,4,256,1024]{2,3,1,0:T(8,128)(2,1)S(1)}, bf16[2,4,256,1024]{2,3,1,0:T(8,128)(2,1)}, u32[]{:S(2)}) copy-start(bf16[2,4,256,1024]{2,3,1,0:T(8,128)(2,1)} %copy-done.1) | copy-start | bytes 12582916
  76.2 4.6 %copy-start.10 = (bf16[1024,1,256]{0,2,1:T(8,128)(2,1)S(1)}, bf16[1024,1,256]{0,2,1:T(8,128)(2,1)}, u32[]{:S(2)}) copy-start(bf16[1024,1,256]{0,2,1:T(8,128)(2,1)} %copy.93) | copy-start | bytes 1572868
  80.8 1.8 copy-start.22
  80.8 3.8 %copy-start.8 = (bf16[256,1024]{0,1:T(8,128)(2,1)S(1)}, bf16[256,1024]{0,1:T(8,128)(2,1)}, u32[]{:S(2)}) copy-start(bf16[256,1024]{0,1:T(8,128)(2,1)} %copy.162) | copy-start | bytes 1572868
  82.6 1.9 copy-start.3
  94.6 212.2 %all-gather.5.cloned.1.call-start = ((), (), s32[]{:S(2)}) async-start(), calls=%async_computation.1 | async-start | bytes 17825792 | tf_op jit(solution)/shard_map/all_gather | solution.py:28
  98.2 267.6 %all-reduce.5.cloned.1.call-start = ((), (), s32[]{:S(2)}) async-start(), calls=%async_computation.2 | async-start | bytes 524288 | tf_op jit(solution)/shard_map/psum | solution.py:149
  104.7 3.7 copy-start.13
  104.7 3.9 %copy-start.24 = (pred[256,256]{1,0:T(8,128)(4,1)S(1)}, pred[256,256]{1,0:T(8,128)(4,1)}, u32[]{:S(2)}) copy-start(pred[256,256]{1,0:T(8,128)(4,1)} %copy.97) | copy-start | bytes 196612
  104.7 4.0 %copy-start.26 = (f32[16,256]{1,0:T(8,128)S(1)}, f32[16,256]{1,0:T(8,128)}, u32[]{:S(2)}) copy-start(f32[16,256]{1,0:T(8,128)} %param.17) | copy-start | bytes 49156
  107.5 4.0 %copy-start.16 = (bf16[256,256]{1,0:T(8,128)(2,1)}, bf16[256,256]{1,0:T(8,128)(2,1)S(1)}, u32[]{:S(2)}) copy-start(bf16[256,256]{1,0:T(8,128)(2,1)S(1)} %convert_reduce_fusion) | copy-start | bytes 393220
  108.7 2.8 copy-start.4
  108.7 2.8 copy-start.9
  111.6 1.7 copy-start.21
  111.6 1.7 copy-start.23
  213.2 102.6 %copy-start.11 = (bf16[256,2048]{0,1:T(8,128)(2,1)S(1)}, bf16[256,2048]{0,1:T(8,128)(2,1)}, u32[]{:S(2)}) copy-start(bf16[256,2048]{0,1:T(8,128)(2,1)} %copy.117) | copy-start | bytes 3145732
  213.2 102.6 %copy-start.18 = (f32[256,16]{0,1:T(8,128)S(1)}, f32[256,16]{0,1:T(8,128)}, u32[]{:S(2)}) copy-start(f32[256,16]{0,1:T(8,128)} %copy-done.17) | copy-start | bytes 49156
  213.2 104.4 %copy-start.14 = (bf16[256,1,256]{2,1,0:T(2,128)(2,1)S(1)}, bf16[256,1,256]{2,1,0:T(2,128)(2,1)}, u32[]{:S(2)}) copy-start(bf16[256,1,256]{2,1,0:T(2,128)(2,1)} %get-tuple-element.32) | copy-start | bytes 393220
Sparse Core Ops, SparseCore 0:
  9.9 41.4 all-gather.2
  94.7 114.0 all-reduce.6
  211.3 95.4 all-gather.4
  320.4 45.2 all-reduce.4
